TPU v7x, 512 devices: a whole 4x8x8 slice. The times are simulated.
512 devices in a mesh: row: 32 (over z_lo, y), col: 16 (over x, z_hi, core).
Axes of the slice: x: 4, y: 8, z: 8 (z_hi: 2, z_lo: 4; z = z_hi * 4 + z_lo), core: 2. Of those that a mesh axis runs over, the one named last changes fastest.
Arguments:
- features: bfloat16 [16, 4096, 128], P('col', 'row'), may hold values from -6 to 6
- weight: bfloat16 [128, 256], replicated, may hold values from -0.5 to 0.5
- tile_values: bfloat16 [32, 16, 32, 128, 128], P('row', 'col'), may hold values from -0.125 to 0.125
- tile_rows: int32 [32, 16, 32], P('row', 'col'), may hold values from 0 to 15
- tile_cols: int32 [32, 16, 32], P('row', 'col'), may hold values from 0 to 31
- tile_count: int32 [32, 16], P('row', 'col'), may hold values from 4 to 32, as said below
- cotangent: bfloat16 [32, 2048, 256], P('row', 'col'), may hold values from -6 to 6
Outputs:
- output: bfloat16 [32, 2048, 256], P('row', 'col')
- grad_features: bfloat16 [16, 4096, 128], P('col', 'row')
- weight_grad: float32 [128, 256], replicated
Inputs may be any that keep to these rules, and one draw needn't show every extreme that they name: Slots at or beyond a cell's tile_count are ignored; some cell is full in every draw. Tile coordinates within a cell may repeat, and repeated tiles add.
All inputs are finite; a program needn't handle non-finite values.
Results may differ from a plain program's by a relative error of at most 0.022.
Values may be sent and summed in bfloat16 or wider, within the bound.
No kernel may reach another device: no remote copies, remote signals or barrier semaphores. Data moves between devices by JAX's collectives and lax.ppermute only.
A program may use at most 64 MiB of HBM per device.

v0:
```python
import jax
import jax.numpy as jnp
from jax import lax
from jax.sharding import PartitionSpec as P


def tile_products(
    tile_block, target_ids, source_ids, tile_total, source, out_blocks, transpose, block_width
):
    source_blocks = source[source_ids]
    if transpose:
        products = jnp.einsum(
            "tij,tif->tjf", tile_block, source_blocks, preferred_element_type=jnp.float32
        )
    else:
        products = jnp.einsum(
            "tij,tjf->tif", tile_block, source_blocks, preferred_element_type=jnp.float32
        )
    slot_ids = jnp.arange(block_width, dtype=jnp.int32)
    live_mask = slot_ids < tile_total
    one_hot = (
        (target_ids[None, :] == jnp.arange(out_blocks, dtype=jnp.int32)[:, None])
        & live_mask[None, :]
    ).astype(jnp.float32)
    return jnp.einsum("rt,tif->rif", one_hot, products, precision=lax.Precision.HIGH)


def spread_tiles(tile_block, target_ids, source_ids, tile_total, source, out_blocks, transpose):
    capacity = tile_block.shape[0]
    return tile_products(
        tile_block, target_ids, source_ids, tile_total, source, out_blocks, transpose, capacity
    )


def on_device(features, weight, tile_values, tile_rows, tile_cols, tile_count, cotangent):
    rows_dev = features.shape[1]
    width_in = features.shape[2]
    tile_size = tile_values.shape[-1]
    row_devices = lax.axis_size("row")
    col_devices = lax.axis_size("col")
    row_tiles = rows_dev * col_devices // tile_size
    col_tiles = rows_dev * row_devices // tile_size
    node_total = rows_dev * row_devices * col_devices
    tile_block = tile_values[0, 0]
    row_ids = tile_rows[0, 0]
    col_ids = tile_cols[0, 0]
    tile_total = tile_count[0, 0]
    gathered = lax.all_gather(features, "row", axis=1, tiled=True)
    col_source = gathered.reshape(col_tiles, tile_size, width_in)
    partial_value = spread_tiles(
        tile_block, row_ids, col_ids, tile_total, col_source, row_tiles, False
    )
    partial_value = partial_value.reshape(row_tiles * tile_size, width_in)
    aggregated = lax.psum_scatter(partial_value, "col", scatter_dimension=0, tiled=True).astype(
        jnp.bfloat16
    )
    pre = jnp.dot(aggregated, weight, preferred_element_type=jnp.float32)
    sigma = jax.nn.sigmoid(pre)
    output = (pre * sigma).astype(jnp.bfloat16)[None]
    slope = sigma * (1.0 + pre * (1.0 - sigma))
    grad_pre = (cotangent[0].astype(jnp.float32) * slope).astype(jnp.bfloat16)
    local_grad = lax.dot_general(
        aggregated, grad_pre, (((0,), (0,)), ((), ())), preferred_element_type=jnp.float32
    )
    weight_grad = lax.psum(local_grad, ("row", "col")) * node_total ** (-0.5)
    full_pre = lax.all_gather(grad_pre, "col", axis=0, tiled=True)
    row_source = lax.dot_general(
        full_pre, weight, (((1,), (1,)), ((), ())), preferred_element_type=jnp.float32
    ).astype(jnp.bfloat16)
    row_source = row_source.reshape(row_tiles, tile_size, width_in)
    partial_back = spread_tiles(
        tile_block, col_ids, row_ids, tile_total, row_source, col_tiles, True
    )
    partial_back = partial_back.reshape(col_tiles * tile_size, width_in)
    grad_features = lax.psum_scatter(
        partial_back.astype(jnp.bfloat16), "row", scatter_dimension=0, tiled=True
    )[None]
    return (output, grad_features, weight_grad)


def solution(mesh):
    placed = (
        P("col", "row", None),
        P(),
        P("row", "col", None, None, None),
        P("row", "col", None),
        P("row", "col", None),
        P("row", "col"),
        P("row", "col", None),
    )
    return jax.shard_map(
        on_device,
        mesh=mesh,
        in_specs=placed,
        out_specs=(P("row", "col", None), P("col", "row", None), P()),
        check_vma=False,
    )
```

profile of v0, /device:TPU:4, one launch (start us, length us, event | category | flops | bytes accessed | tf_op | source)
XLA Modules:
  0.0 752.0 jit_solution(3322477829426455184)
XLA Ops:
  7.2 0.0 copy-start
  7.2 0.0 all-gather.3.cloned.1.call-start
  7.2 0.7 all-gather.3.cloned.1.call-update
  7.9 0.0 reduce-scatter.3.cloned.1.call-start
  8.6 0.7 fusion.27
  9.3 158.5 %all-gather.3.cloned.1.call-done = bf16[1,4096,128]{2,1,0:T(8,128)(2,1)} async-done(((bf16[1,128,128]{2,1,0:T(8,128)(2,1)}), bf16[1,4096,128]{2,1,0:T(8,128)(2,1)}) %all-gather.3.cloned.1.call-update) | async-done | bytes 1048592 | tf_op jit(solution)/shard_map/all_gather | solution.py:48
  167.8 2.9 gather_fusion
  170.7 2.1 fusion.9
  172.8 2.1 copy.12
  174.9 2.1 fusion.2
  176.9 0.0 copy-start.1
  177.0 1.3 copy.10
  178.3 0.0 reduce-scatter.3.cloned.1.call-update
  178.3 0.0 all-gather.5.cloned.1.call-start
  178.3 82.4 %reduce-scatter.3.cloned.1.call-done = f32[128,128]{1,0:T(8,128)} async-done(((f32[2048,128]{1,0:T(8,128)}), f32[128,128]{1,0:T(8,128)}) %reduce-scatter.3.cloned.1.call-update) | async-done | bytes 65552 | tf_op jit(solution)/shard_map/reduce_scatter | solution.py:54
  260.7 1.7 fusion.11
  262.4 0.0 all-gather.5.cloned.1.call-update
  262.4 0.0 all-reduce.2.cloned.1.call-start
  262.5 1.7 fusion.13
  264.2 0.0 all-reduce.2.cloned.1.call-update
  264.3 0.0 reduce-scatter.5.cloned.1.call-start
  264.3 57.5 %all-gather.5.cloned.1.call-done = bf16[2048,256]{1,0:T(8,128)(2,1)} async-done(((bf16[128,256]{1,0:T(8,128)(2,1)}), bf16[2048,256]{1,0:T(8,128)(2,1)}) %all-gather.5.cloned.1.call-update) | async-done | bytes 1048592 | tf_op jit(solution)/shard_map/all_gather | solution.py:66
  321.8 1.7 convolution_convert_fusion
  323.5 0.8 gather_fusion.1
  324.2 1.9 fusion.7
  326.1 2.4 copy.13
  328.5 0.7 fusion.4
  329.2 1.4 copy.11
  330.6 0.0 reduce-scatter.5.cloned.1.call-update
  330.6 253.5 %all-reduce.2.cloned.1.call-done = f32[128,256]{1,0:T(8,128)} async-done(((f32[128,256]{1,0:T(8,128)}), f32[128,256]{1,0:T(8,128)}) %all-reduce.2.cloned.1.call-update) | async-done | bytes 131088 | tf_op jit(solution)/shard_map/psum | solution.py:65
  584.2 1.6 broadcast_multiply_fusion
  585.7 159.7 %reduce-scatter.5.cloned.1.call-done = bf16[128,128]{1,0:T(8,128)(2,1)} async-done(((bf16[4096,128]{1,0:T(8,128)(2,1)}), bf16[128,128]{1,0:T(8,128)(2,1)}) %reduce-scatter.5.cloned.1.call-update) | async-done | bytes 32784 | tf_op jit(solution)/shard_map/reduce_scatter | solution.py:75
  (12 shorter events, 0.0 us)
Async XLA Ops:
  7.2 163.5 %copy-start = (bf16[1,1,32,128,128]{4,3,2,1,0:T(8,128)(2,1)S(1)}, bf16[1,1,32,128,128]{4,3,2,1,0:T(8,128)(2,1)}, u32[]{:S(2)}) copy-start(bf16[1,1,32,128,128]{4,3,2,1,0:T(8,128)(2,1)} %param.9) | copy-start | bytes 3145732
  7.2 160.6 %all-gather.3.cloned.1.call-start = ((), (), s32[]{:S(2)}) async-start(), calls=%async_computation.2 | async-start | bytes 1081344 | tf_op jit(solution)/shard_map/all_gather | solution.py:48
  7.9 252.8 %reduce-scatter.3.cloned.1.call-start = ((), (), s32[]{:S(2)}) async-start(), calls=%async_computation.3 | async-start | bytes 1114112 | tf_op jit(solution)/shard_map/reduce_scatter | solution.py:54
  172.8 2.1 copy-start.2
  176.9 83.8 %copy-start.1 = (bf16[128,256]{1,0:T(8,128)(2,1)S(1)}, bf16[128,256]{1,0:T(8,128)(2,1)}, u32[]{:S(2)}) copy-start(bf16[128,256]{1,0:T(8,128)(2,1)} %param.8) | copy-start | bytes 196612
  177.0 83.8 %copy-start.4 = (bf16[1,128,256]{2,1,0:T(8,128)(2,1)S(1)}, bf16[1,128,256]{2,1,0:T(8,128)(2,1)}, u32[]{:S(2)}) copy-start(bf16[1,128,256]{2,1,0:T(8,128)(2,1)} %param.13) | copy-start | bytes 196612
  178.3 143.5 %all-gather.5.cloned.1.call-start = ((), (), s32[]{:S(2)}) async-start(), calls=%async_computation.4 | async-start | bytes 1114112 | tf_op jit(solution)/shard_map/all_gather | solution.py:66
  262.4 321.7 %all-reduce.2.cloned.1.call-start = ((), (), s32[]{:S(2)}) async-start(), calls=%async_computation.6 | async-start | bytes 262144 | tf_op jit(solution)/shard_map/psum | solution.py:65
  264.3 481.2 %reduce-scatter.5.cloned.1.call-start = ((), (), s32[]{:S(2)}) async-start(), calls=%async_computation.5 | async-start | bytes 1081344 | tf_op jit(solution)/shard_map/reduce_scatter | solution.py:75
  326.1 2.4 copy-start.3
Sparse Core Ops, SparseCore 0:
  10.1 157.6 all-gather.2
  178.4 82.2 reduce-scatter.2
  264.5 57.2 all-gather.4
  328.0 256.1 all-reduce.1
  587.4 158.0 reduce-scatter.4
where the time goes:
time: 752 us
  waiting for transfers between devices  712 us (95%)
  between operations  14.5 us (2%)
  matrix products  11.8 us (2%)
  local copies, waits for them, and re-layouts  10.8 us (1%)
    psum x1, waiting for transfers between devices, on_device(): weight_grad = lax.psum(local_grad, ('row', 'col')) * node_total ** (-0.5)  254 us
    reduce_scatter x1, waiting for transfers between devices, on_device(): lax.psum_scatter(partial_back.astype(jnp.bfloat16), 'row', scatter_dimens...  160 us
    all_gather x1, waiting for transfers between devices, on_device(): gathered = lax.all_gather(features, 'row', axis=1, tiled=True)  159 us
    reduce_scatter x1, waiting for transfers between devices, on_device(): lax.psum_scatter(partial_value, 'col', scatter_dimension=0, tiled=True)  82.4 us
    all_gather x1, waiting for transfers between devices, on_device(): full_pre = lax.all_gather(grad_pre, 'col', axis=0, tiled=True)  57.5 us
  transfers between devices with their start and end apart: 5, of which 5 were waited for; matrix products, arithmetic and copies ran while one was open for 2% of the time, Pallas kernels for 0%

commit v1 on v0

--- a/solution.py
+++ b/solution.py
@@ -45,7 +45,14 @@
     row_ids = tile_rows[0, 0]
     col_ids = tile_cols[0, 0]
     tile_total = tile_count[0, 0]
-    gathered = lax.all_gather(features, "row", axis=1, tiled=True)
+
+    def _use_roots(array_here, comm_axis):
+        t1 = jnp.stack(lax.axis_size(comm_axis) * [array_here], 0)
+        b_next = lax.all_to_all(t1, axis_name=comm_axis, split_axis=0, concat_axis=0)
+        all_values = jnp.concatenate(b_next, 1)
+        return all_values
+
+    gathered = _use_roots(features, "row")
     col_source = gathered.reshape(col_tiles, tile_size, width_in)
     partial_value = spread_tiles(
         tile_block, row_ids, col_ids, tile_total, col_source, row_tiles, False

time: 752 us -> 638 us (0.85)
  waiting for transfers between devices: 712 us -> 585 us
  starting transfers between devices: 0.2 us -> 13.1 us
    all_gather x1 -> x0, waiting for transfers between devices: 159 us -> none  [on_device(): gathered = lax.all_gather(features, 'row', axis=1, tiled=True)]
    all_to_all x0 -> x1, waiting for transfers between devices: none -> 28.5 us  [_use_roots(): lax.all_to_all(t1, axis_name=comm_axis, split_axis=0, concat_axis=0)]
    all_to_all x0 -> x1, starting transfers between devices: none -> 12.9 us  [_use_roots(): lax.all_to_all(t1, axis_name=comm_axis, split_axis=0, concat_axis=0)]
where the time goes in v1:
time: 638 us
  waiting for transfers between devices  585 us (92%)
  between operations  14.5 us (2%)
  starting transfers between devices  13.1 us (2%)
  matrix products  11.8 us (2%)
  local copies, waits for them, and re-layouts  11.6 us (2%)
    psum x1, waiting for transfers between devices, on_device(): weight_grad = lax.psum(local_grad, ('row', 'col')) * node_total ** (-0.5)  254 us
    reduce_scatter x1, waiting for transfers between devices, on_device(): lax.psum_scatter(partial_back.astype(jnp.bfloat16), 'row', scatter_dimens...  160 us
    reduce_scatter x1, waiting for transfers between devices, on_device(): lax.psum_scatter(partial_value, 'col', scatter_dimension=0, tiled=True)  85.5 us
    all_gather x1, waiting for transfers between devices, on_device(): full_pre = lax.all_gather(grad_pre, 'col', axis=0, tiled=True)  57.4 us
    all_to_all x1, waiting for transfers between devices, _use_roots(): lax.all_to_all(t1, axis_name=comm_axis, split_axis=0, concat_axis=0)  28.5 us
    all_to_all x1, starting transfers between devices, _use_roots(): lax.all_to_all(t1, axis_name=comm_axis, split_axis=0, concat_axis=0)  12.9 us
  transfers between devices with their start and end apart: 5, of which 5 were waited for; matrix products, arithmetic and copies ran while one was open for 2% of the time, Pallas kernels for 0%

profile of v1, /device:TPU:4, one launch (start us, length us, event | category | flops | bytes accessed | tf_op | source)
XLA Modules:
  0.0 637.5 jit_solution(16400471065144516666)
XLA Ops:
  7.2 0.0 copy-start
  7.2 2.1 stack.2
  9.2 12.9 %all-to-all-start = ((bf16[32,1,128,128]{3,2,1,0:T(8,128)(2,1)}), bf16[32,1,128,128]{3,2,1,0:T(8,128)(2,1)S(1)}, u32[]{:S(2)}, u32[]{:S(2)}) async-start(bf16[32,1,128,128]{3,2,1,0:T(8,128)(2,1)} %stack.2), calls=%async_computation | async-start | bytes 2097152 | tf_op jit(solution)/shard_map/all_to_all | solution.py:51
  22.2 0.0 reduce-scatter.3.cloned.1.call-start
  22.9 28.5 %all-to-all-done = bf16[32,1,128,128]{3,2,1,0:T(8,128)(2,1)S(1)} async-done(((bf16[32,1,128,128]{3,2,1,0:T(8,128)(2,1)}), bf16[32,1,128,128]{3,2,1,0:T(8,128)(2,1)S(1)}, u32[]{:S(2)}, u32[]{:S(2)}) %all-to-all-start) | async-done | bytes 1048608 | tf_op jit(solution)/shard_map/all_to_all | solution.py:51
  51.4 1.6 gather_fusion
  53.0 2.1 fusion.9
  55.2 2.1 copy.12
  57.2 2.1 fusion.2
  59.3 0.0 copy-start.1
  59.3 0.0 copy-start.4
  59.3 1.3 copy.10
  60.6 0.0 reduce-scatter.3.cloned.1.call-update
  60.6 0.0 all-gather.2.cloned.1.call-start
  60.7 85.5 %reduce-scatter.3.cloned.1.call-done = f32[128,128]{1,0:T(8,128)} async-done(((f32[2048,128]{1,0:T(8,128)}), f32[128,128]{1,0:T(8,128)}) %reduce-scatter.3.cloned.1.call-update) | async-done | bytes 65552 | tf_op jit(solution)/shard_map/reduce_scatter | solution.py:61
  146.2 1.7 fusion.11
  147.9 0.0 all-gather.2.cloned.1.call-update
  147.9 0.0 all-reduce.2.cloned.1.call-start
  148.0 1.7 fusion.13
  149.7 0.0 all-reduce.2.cloned.1.call-update
  149.8 0.0 reduce-scatter.5.cloned.1.call-start
  149.8 57.4 %all-gather.2.cloned.1.call-done = bf16[2048,256]{1,0:T(8,128)(2,1)} async-done(((bf16[128,256]{1,0:T(8,128)(2,1)}), bf16[2048,256]{1,0:T(8,128)(2,1)}) %all-gather.2.cloned.1.call-update) | async-done | bytes 1048592 | tf_op jit(solution)/shard_map/all_gather | solution.py:73
  207.2 1.7 convolution_convert_fusion
  208.9 0.8 gather_fusion.1
  209.6 1.9 fusion.7
  211.5 2.4 copy.13
  213.9 0.7 fusion.4
  214.6 1.4 copy.11
  216.0 0.0 reduce-scatter.5.cloned.1.call-update
  216.0 253.7 %all-reduce.2.cloned.1.call-done = f32[128,256]{1,0:T(8,128)} async-done(((f32[128,256]{1,0:T(8,128)}), f32[128,256]{1,0:T(8,128)}) %all-reduce.2.cloned.1.call-update) | async-done | bytes 131088 | tf_op jit(solution)/shard_map/psum | solution.py:72
  469.7 1.6 broadcast_multiply_fusion
  471.3 159.7 %reduce-scatter.5.cloned.1.call-done = bf16[128,128]{1,0:T(8,128)(2,1)} async-done(((bf16[4096,128]{1,0:T(8,128)(2,1)}), bf16[128,128]{1,0:T(8,128)(2,1)}) %reduce-scatter.5.cloned.1.call-update) | async-done | bytes 32784 | tf_op jit(solution)/shard_map/reduce_scatter | solution.py:82
  (12 shorter events, 0.0 us)
Async XLA Ops:
  7.2 45.9 %copy-start = (bf16[1,1,32,128,128]{4,3,2,1,0:T(8,128)(2,1)S(1)}, bf16[1,1,32,128,128]{4,3,2,1,0:T(8,128)(2,1)}, u32[]{:S(2)}) copy-start(bf16[1,1,32,128,128]{4,3,2,1,0:T(8,128)(2,1)} %param.9) | copy-start | bytes 3145732
  7.2 15.7 %copy-start.3 = (s32[1,1,32]{2,1,0:T(1,128)S(1)}, s32[1,1,32]{2,1,0:T(1,128)}, u32[]{:S(2)}) copy-start(s32[1,1,32]{2,1,0:T(1,128)} %param.11) | copy-start | bytes 388
  9.2 42.1 %all-to-all-start = ((bf16[32,1,128,128]{3,2,1,0:T(8,128)(2,1)}), bf16[32,1,128,128]{3,2,1,0:T(8,128)(2,1)S(1)}, u32[]{:S(2)}, u32[]{:S(2)}) async-start(bf16[32,1,128,128]{3,2,1,0:T(8,128)(2,1)} %stack.2), calls=%async_computation | async-start | bytes 2097152 | tf_op jit(solution)/shard_map/all_to_all | solution.py:51
  22.2 124.0 %reduce-scatter.3.cloned.1.call-start = ((), (), s32[]{:S(2)}) async-start(), calls=%async_computation.3 | async-start | bytes 1114112 | tf_op jit(solution)/shard_map/reduce_scatter | solution.py:61
  55.2 2.1 copy-start.2
  59.3 86.9 %copy-start.1 = (bf16[128,256]{1,0:T(8,128)(2,1)S(1)}, bf16[128,256]{1,0:T(8,128)(2,1)}, u32[]{:S(2)}) copy-start(bf16[128,256]{1,0:T(8,128)(2,1)} %param.8) | copy-start | bytes 196612
  59.3 86.9 %copy-start.4 = (bf16[1,128,256]{2,1,0:T(8,128)(2,1)S(1)}, bf16[1,128,256]{2,1,0:T(8,128)(2,1)}, u32[]{:S(2)}) copy-start(bf16[1,128,256]{2,1,0:T(8,128)(2,1)} %param.13) | copy-start | bytes 196612
  60.6 146.6 %all-gather.2.cloned.1.call-start = ((), (), s32[]{:S(2)}) async-start(), calls=%async_computation.4 | async-start | bytes 1114112 | tf_op jit(solution)/shard_map/all_gather | solution.py:73
  147.9 321.8 %all-reduce.2.cloned.1.call-start = ((), (), s32[]{:S(2)}) async-start(), calls=%async_computation.6 | async-start | bytes 262144 | tf_op jit(solution)/shard_map/psum | solution.py:72
  149.8 481.2 %reduce-scatter.5.cloned.1.call-start = ((), (), s32[]{:S(2)}) async-start(), calls=%async_computation.5 | async-start | bytes 1081344 | tf_op jit(solution)/shard_map/reduce_scatter | solution.py:82
Sparse Core Ops, SparseCore 0:
  60.8 85.4 reduce-scatter.2
  150.0 57.1 all-gather.1
  213.6 256.1 all-reduce.1
  472.9 158.0 reduce-scatter.4
